TPU v7x, 32 devices: a whole 2x2x4 slice. The times are simulated.
32 devices in a mesh: rows: 8 (over z, y), grp: 4 (over x, core).
Axes of the slice: x: 2, y: 2, z: 4, core: 2. Of those that a mesh axis runs over, the one named last changes fastest.
Arguments:
- cholesky_vectors: bfloat16 [65536, 2048], P(('rows', 'grp'))
- integral_columns: float32 [65536, 64], P(('rows', 'grp'))
- residual_diag: float32 [65536], P(('rows', 'grp')), may hold values from 40 to 120
- slot_pair_block: int32 [512], P(('rows', 'grp')), may hold values from 0 to 511, as said below
- block_live: int32 [512], P(('rows', 'grp')), may hold values from 0 to 1, as said below
- pivots: int32 [64], replicated, may hold values from 0 to 65535, as said below
Outputs:
- new_columns: float32 [65536, 64], P(('rows', 'grp'))
- relative_diag: float32 [65536], P(('rows', 'grp'))
- peak: float32 [], replicated
Inputs may be any that keep to these rules, and one draw needn't show every extreme that they name: `slot_pair_block`: each block number appears once. `block_live`: slots s * 16 to s * 16 + 15 are those of device s; each device has 1 to 12 surviving slots, and some device has exactly 12. Distinct; every pivot lies in a surviving slot; each device's slots hold at most 2 pivots, and some device holds exactly 2.
All inputs are finite; a program needn't handle non-finite values.
Results may differ from a plain program's by a relative error of at most 0.0003.
Values sent between devices are 32-bit elements; how exact they have to be, the bound alone decides.
A program may use at most 64 MiB of HBM per device.

v0:
```python
import jax
import jax.numpy as jnp
from jax import lax
from jax.sharding import PartitionSpec as P


def on_device(
    cholesky_vectors, integral_columns, residual_diag, slot_pair_block, block_live, pivots
):
    slots = slot_pair_block.shape[0]
    total_rows = cholesky_vectors.shape[0]
    block_rows = total_rows // slots
    piv_count = pivots.shape[0]
    holders = lax.axis_size("rows") * lax.axis_size("grp")
    per_holder = max(1, piv_count // holders)
    pivot_group = pivots // block_rows
    pivot_offset = pivots % block_rows
    matches = pivot_group[:, None] == slot_pair_block[None, :]
    is_owned = jnp.any(matches, axis=1)
    local_slot = jnp.argmax(matches.astype(jnp.int32), axis=1)
    local_row = local_slot * block_rows + pivot_offset
    own_vectors = jnp.where(
        is_owned[:, None], cholesky_vectors[local_row], jnp.zeros((), jnp.bfloat16)
    )
    own_block = jnp.where(is_owned[:, None], integral_columns[local_row], 0.0)
    pivot_rank = jnp.cumsum(is_owned.astype(jnp.int32)) - 1
    selector = (pivot_rank[None, :] == jnp.arange(per_holder)[:, None]) & is_owned[None, :]
    packed_vectors = jnp.dot(
        selector.astype(jnp.bfloat16), own_vectors, preferred_element_type=jnp.float32
    )
    packed_block = jnp.dot(selector.astype(jnp.float32), own_block, precision=lax.Precision.HIGHEST)
    packed_ids = jnp.where(
        jnp.any(selector, axis=1),
        jnp.sum(jnp.where(selector, jnp.arange(piv_count)[None, :], 0), axis=1),
        -1,
    )
    all_vectors, all_blocks, all_ids = (
        lax.all_gather(packed_vectors, ("rows", "grp"), axis=0, tiled=True),
        lax.all_gather(packed_block, ("rows", "grp"), axis=0, tiled=True),
        lax.all_gather(packed_ids, ("rows", "grp"), axis=0, tiled=True),
    )
    placing = (all_ids[None, :] == jnp.arange(piv_count)[:, None]).astype(jnp.float32)
    picked_wide = jnp.dot(placing, all_vectors, precision=lax.Precision.HIGHEST)
    pivot_block = jnp.dot(placing, all_blocks, precision=lax.Precision.HIGHEST)
    gram = jnp.dot(picked_wide, picked_wide.T, precision=lax.Precision.HIGHEST)
    lower_factor = jnp.linalg.cholesky(pivot_block - gram)
    picked = picked_wide.astype(jnp.bfloat16)
    row_live = jnp.repeat(block_live, block_rows) > 0
    remain = integral_columns - jnp.dot(
        cholesky_vectors, picked.T, preferred_element_type=jnp.float32
    )
    columns = lax.linalg.triangular_solve(
        lower_factor, remain, left_side=False, lower=True, transpose_a=True
    )
    columns = jnp.where(row_live[:, None], columns, 0.0)
    updated = jnp.where(row_live, residual_diag - jnp.sum(columns * columns, axis=1), residual_diag)
    columns, updated = (columns, updated)
    is_pivot = jnp.any(
        (local_row[:, None] == jnp.arange(total_rows)[None, :]) & is_owned[:, None], axis=0
    )
    updated = jnp.where(is_pivot, 0.0, updated)
    local_peak = jnp.max(jnp.where(row_live, updated, 0.0))
    peak = lax.pmax(local_peak, ("rows", "grp"))
    return (columns, updated / peak, peak)


def solution(mesh):
    in_specs = (
        P(("rows", "grp"), None),
        P(("rows", "grp"), None),
        P(("rows", "grp")),
        P(("rows", "grp")),
        P(("rows", "grp")),
        P(),
    )
    out_specs = (P(("rows", "grp"), None), P(("rows", "grp")), P())
    return jax.shard_map(
        on_device, mesh=mesh, in_specs=in_specs, out_specs=out_specs, check_vma=False
    )
```

profile of v0, /device:TPU:0, one launch (start us, length us, event | category | flops | bytes accessed | tf_op | source)
XLA Modules:
  0.0 193.5 jit_solution(14119491912677781188)
XLA Ops:
  0.6 0.0 copy-start
  0.6 0.7 and_select_fusion.1
  1.4 0.7 compare_reduce_fusion
  2.1 0.1 copy.24
  2.2 0.1 reduce-window.8
  2.3 0.1 add_reduce_fusion
  2.4 0.1 fusion.22
  2.5 0.1 select_reduce_fusion.2
  2.7 0.1 select_dynamic-update-slice_fusion
  2.8 42.0 %all-reduce = s32[64]{0:T(128)S(1)} all-reduce(s32[64]{0:T(128)S(1)} %select_dynamic-update-slice_fusion), channel_id=1, replica_groups=mesh['rows'=8,'grp'=4] {'rows','grp'}, use_global_device_ids=true, to_apply=%add | all-reduce | flops 64 | bytes 512
  44.7 1.3 fusion.17
  46.0 0.7 compare_select_fusion
  46.7 5.4 %gather_fusion = bf16[64,2048]{1,0:T(8,128)(2,1)S(1)} fusion(bf16[2048,2048]{1,0:T(8,128)(2,1)} %param.6, s32[1024]{0:T(1024)S(1)} %pad_clamp_fusion), kind=kCustom, calls=%fused_computation | custom fusion | bytes 524544 | tf_op jit(solution)/shard_map/gather | solution.py:23
  52.1 0.0 copy-start.2
  52.1 0.2 convolution_bitcast_fusion.1
  52.4 41.7 %all-gather = f32[32,2,2048]{2,1,0:T(2,128)S(1)} all-gather(f32[1,2,2048]{2,1,0:T(2,128)S(1)} %convolution_bitcast_fusion.1), channel_id=1, replica_groups=mesh['rows'=8,'grp'=4] {'rows','grp'}, dimensions={0}, use_global_device_ids=true | all-gather | bytes 540672 | tf_op jit(solution)/shard_map/all_gather | solution.py:38
  94.0 0.0 copy-start.1
  94.0 0.4 reshape.83
  94.4 0.4 fusion.12
  94.8 1.4 copy.25
  96.2 0.6 gather_fusion.1
  96.8 0.2 convolution_bitcast_fusion.2
  97.0 36.7 %all-gather.1 = f32[32,2,64]{2,1,0:T(2,128)S(1)} all-gather(f32[1,2,64]{2,1,0:T(2,128)S(1)} %convolution_bitcast_fusion.2), channel_id=1, replica_groups=mesh['rows'=8,'grp'=4] {'rows','grp'}, dimensions={0}, use_global_device_ids=true | all-gather | bytes 16896 | tf_op jit(solution)/shard_map/all_gather | solution.py:39
  133.7 0.2 fusion.11
  133.9 0.6 convolution_subtract_fusion
  134.5 0.1 copy.28
  134.6 5.8 %cholesky.15 = f32[64,64]{1,0:T(8,128)S(1)} custom-call(f32[64,64]{1,0:T(8,128)S(1)} %fusion.9), custom_call_target="Cholesky" | custom-call | tf_op jit(solution)/shard_map/jit(cholesky)/cholesky | solution.py:46
  140.5 0.6 compare_reduce_fusion.1
  141.1 0.7 fusion.7
  141.8 4.9 %custom-call.6 = f32[1,64,64]{1,2,0:T(8,128)S(1)} custom-call(f32[1,64,64]{2,1,0:T(8,128)S(1)} %fusion.7), custom_call_target="InvertDiagBlocksLowerTriangular" | custom-call | tf_op jit(solution)/shard_map/triangular_solve | solution.py:52
  146.7 0.0 copy-done
  146.7 6.0 %fusion = f32[2048,64]{0,1:T(8,128)S(1)} fusion(f32[2048,64]{0,1:T(8,128)S(1)} %copy-done, bf16[2048,2048]{1,0:T(8,128)(2,1)} %param.6, f32[64,2048]{1,0:T(8,128)S(1)} %fusion.12), kind=kOutput, calls=%fused_computation.3 | convolution fusion | flops 537133056 | bytes 9961472 | tf_op jit(solution)/shard_map/dot_general | solution.py:49
  152.7 0.0 copy-done.2
  152.8 0.1 broadcast_bitcast_fusion
  152.8 1.4 multiply_reduce_fusion
  154.3 0.2 fusion.2
  154.4 0.0 copy-done.1
  154.4 0.7 select_reduce_fusion.1
  155.1 37.1 %pmax.7 = f32[]{:T(128)} all-reduce(f32[]{:T(128)} %select_reduce_fusion.1), channel_id=1, replica_groups=mesh['rows'=8,'grp'=4] {'rows','grp'}, use_global_device_ids=true, to_apply=%region_10.11 | all-reduce | flops 1 | bytes 8 | tf_op jit(solution)/shard_map/pmax | solution.py:63
  192.2 1.3 broadcast_divide_fusion
  (6 shorter events, 0.1 us)
Async XLA Ops:
  0.6 146.1 %copy-start = (f32[2048,64]{0,1:T(8,128)S(1)}, f32[2048,64]{0,1:T(8,128)}, u32[]{:S(2)}) copy-start(f32[2048,64]{0,1:T(8,128)} %param.7) | copy-start | bytes 1572868
  52.1 100.6 %copy-start.2 = (s32[16]{0:T(128)S(1)}, s32[16]{0:T(128)}, u32[]{:S(2)}) copy-start(s32[16]{0:T(128)} %param.10) | copy-start | bytes 196
  94.0 60.4 %copy-start.1 = (f32[2048]{0:T(1024)S(1)}, f32[2048]{0:T(1024)}, u32[]{:S(2)}) copy-start(f32[2048]{0:T(1024)} %param.8) | copy-start | bytes 24580
where the time goes:
time: 195 us; the launch traced here: 194 us
  blocking collectives  157 us (81%)
  other arithmetic  18.2 us (9%)
  matrix products  9.07 us (5%)
  local copies, waits for them, and re-layouts  8.06 us (4%)
    unnamed x1, blocking collectives  42 us
    all_gather x1, blocking collectives, on_device(): lax.all_gather(packed_vectors, ('rows', 'grp'), axis=0, tiled=True)  41.7 us
    pmax x1, blocking collectives, on_device(): peak = lax.pmax(local_peak, ('rows', 'grp'))  37.1 us
    all_gather x1, blocking collectives, on_device(): lax.all_gather(packed_block, ('rows', 'grp'), axis=0, tiled=True)  36.7 us
    another operation x3, other arithmetic, on_device(): lower_factor = jnp.linalg.cholesky(pivot_block - gram)  6.52 us
    dot_general x1, matrix products, on_device(): jnp.dot(cholesky_vectors, picked.T, preferred_element_type=jnp.float32)  6.04 us
    another operation x2, other arithmetic, on_device(): lax.linalg.triangular_solve(lower_factor, remain, left_side=False, lower=...  5.55 us
    gather x1, local copies, waits for them, and re-layouts, on_device(): cholesky_vectors[local_row]  5.45 us

commit v1 on v0

v1 whole, which is shorter than its diff:
```python
import functools

import jax
import jax.numpy as jnp
from jax import lax
from jax.experimental import pallas as pl
from jax.experimental.pallas import tpu as pltpu
from jax.sharding import PartitionSpec as P

MESH = pl.DeviceIdType.MESH
LANES = 128


def step_kernel(
    sizes, vec_hbm, col_hbm, res_ref, slot_ref, live_ref, piv_ref,
    new_hbm, rel_ref, peak_ref,
    vec, col, new, send, got, mine, tops, sums, marks,
    vec_sem, col_sem, own_sem, send_sem, chip_sem, core_sem, top_send, top_recv, out_sem,
):
    n_rows, n_grp, per, block, rows_sent, part = sizes
    n = n_rows * n_grp
    total, depth = vec.shape
    slots = total // block
    piv = col.shape[0]
    chunks = depth // LANES
    parts = total // part
    my_row, my_grp = lax.axis_index("rows"), lax.axis_index("grp")
    me = my_row * n_grp + my_grp
    side = lax.rem(my_grp, 2)
    partner_grp = my_grp + 1 - 2 * side
    half = n // 2
    my_chip = me // 2
    over_first = (((0,), (0,)), ((), ()))
    over_last = (((1,), (1,)), ((), ()))

    def place(flat):
        return (flat // n_grp, lax.rem(flat, n_grp))

    def dot_t(a, b):
        return lax.dot_general(a, b, over_last, preferred_element_type=jnp.float32)

    def split(x):
        hi = x.astype(jnp.bfloat16)
        return hi, x - hi.astype(jnp.float32)

    col_copy = pltpu.make_async_copy(col_hbm, col, col_sem)
    col_copy.start()
    vec_copies = [
        pltpu.make_async_copy(
            vec_hbm.at[pl.ds(i * part, part), :], vec.at[pl.ds(i * part, part), :], vec_sem.at[i]
        )
        for i in range(parts)
    ]
    for copy in vec_copies:
        copy.start()

    barrier = pltpu.get_barrier_semaphore()

    def greet(t, carry):
        pl.semaphore_signal(
            barrier, inc=1, device_id=place(lax.rem(me + t, n)), device_id_type=MESH
        )
        return carry

    lax.fori_loop(1, n, greet, 0)

    def iota(shape, axis):
        return lax.broadcasted_iota(jnp.int32, shape, axis)

    def upright(row, size):
        return jnp.sum(
            jnp.where(iota((size, size), 0) == iota((size, size), 1), row, 0), axis=1, keepdims=True
        )

    piv_row = piv_ref[...]
    slot_row = slot_ref[...]
    piv_col = upright(piv_row, piv)
    slot_col = upright(slot_row, slots)
    live_col = upright(live_ref[...], slots)
    group_col, offset_col = piv_col // block, lax.rem(piv_col, block)
    match = jnp.where(group_col == slot_row, 1, 0)
    owned_col = jnp.max(match, axis=1, keepdims=True)
    owned_row = jnp.max(jnp.where(slot_col == piv_row // block, 1, 0), axis=0, keepdims=True)
    before = jnp.where(iota((piv, piv), 0) < iota((piv, piv), 1), owned_col, 0)
    rank_row = jnp.sum(before, axis=0, keepdims=True)
    selector = jnp.where((rank_row == iota((8, piv), 0)) & (owned_row > 0), 1.0, 0.0)
    ids = (
        jnp.sum(selector * (iota((8, piv), 1) + 1).astype(jnp.float32), axis=1, keepdims=True) - 1.0
    )
    selector = selector.astype(jnp.bfloat16)
    hot = []
    here = offset_col == iota((piv, block), 1)
    for s in range(slots):
        at_s = jnp.where(here, match[:, s : s + 1], 0).astype(jnp.float32)
        marks[s : s + 1, :] = jnp.max(at_s, axis=0, keepdims=True)
        hot.append(jnp.dot(selector, at_s.astype(jnp.bfloat16), preferred_element_type=jnp.float32))
    hot = jnp.concatenate(hot, axis=1).astype(jnp.bfloat16)

    send[...] = jnp.zeros_like(send)
    own = jnp.zeros((8, depth), jnp.float32)
    for i in range(parts):
        vec_copies[i].wait()
        at = slice(i * part, (i + 1) * part)
        own = own + jnp.dot(hot[:, at], vec[at, :], preferred_element_type=jnp.float32)
    col_copy.wait()
    col_hi, rest = split(col[...])
    col_mid, rest = split(rest)
    own_col = dot_t(hot, col_hi) + (dot_t(hot, col_mid) + dot_t(hot, rest.astype(jnp.bfloat16)))
    aside = jnp.concatenate([own_col, jnp.broadcast_to(ids, (8, piv))], axis=1)
    for j in range(per):
        for c in range(chunks):
            send[j * chunks + c : j * chunks + c + 1, :] = own[
                j : j + 1, c * LANES : (c + 1) * LANES
            ]
        send[per * chunks + j : per * chunks + j + 1, 0 : 2 * piv] = aside[j : j + 1, :]

    pl.semaphore_wait(barrier, n - 1)

    def slot_of(flat):
        return got.at[pl.ds(pl.multiple_of(flat * rows_sent, 8), rows_sent), :]

    own_copy = pltpu.make_async_copy(send, slot_of(me), own_sem)
    own_copy.start()

    def to_chip(chip):
        flat = chip * 2 + side
        return pltpu.make_async_remote_copy(
            src_ref=send, dst_ref=slot_of(me), send_sem=send_sem, recv_sem=chip_sem.at[my_chip],
            device_id=place(flat), device_id_type=MESH,
        )

    def send_chip(t, carry):
        to_chip(lax.rem(my_chip + t, half)).start()
        return carry

    lax.fori_loop(1, half, send_chip, 0)
    pltpu.make_async_remote_copy(
        src_ref=send, dst_ref=slot_of(me), send_sem=send_sem, recv_sem=core_sem,
        device_id=(my_row, partner_grp), device_id_type=MESH,
    ).start()

    def relay(t, carry):
        chip = lax.rem(my_chip + half - t, half)
        flat = chip * 2 + side
        pltpu.make_async_remote_copy(
            src_ref=send, dst_ref=slot_of(flat), send_sem=send_sem, recv_sem=chip_sem.at[chip],
            device_id=(my_row, partner_grp), device_id_type=MESH,
        ).wait_recv()
        pltpu.make_async_remote_copy(
            src_ref=slot_of(flat), dst_ref=slot_of(flat), send_sem=send_sem, recv_sem=core_sem,
            device_id=(my_row, partner_grp), device_id_type=MESH,
        ).start()
        return carry

    lax.fori_loop(1, half, relay, 0)
    half_ref = got.at[pl.ds(0, half * rows_sent), :]
    own_copy.wait()
    pltpu.make_async_remote_copy(
        src_ref=half_ref, dst_ref=half_ref, send_sem=send_sem, recv_sem=core_sem,
        device_id=(my_row, partner_grp), device_id_type=MESH,
    ).wait_recv()

    arrived = jnp.concatenate(
        [
            jnp.concatenate(
                [
                    got[pl.ds(j * chunks + c, n, stride=rows_sent), :].astype(jnp.bfloat16)
                    for c in range(chunks)
                ],
                axis=1,
            )
            for j in range(per)
        ],
        axis=0,
    )
    aside = jnp.concatenate(
        [got[pl.ds(per * chunks + j, n, stride=rows_sent), :] for j in range(per)], axis=0
    )
    order = lax.broadcasted_iota(jnp.int32, (n * per, piv), 1).astype(jnp.float32)
    placing = jnp.where(aside[:, piv : 2 * piv] == order, 1.0, 0.0)
    picked = lax.dot_general(
        placing.astype(jnp.bfloat16), arrived, over_first, preferred_element_type=jnp.float32
    ).astype(jnp.bfloat16)
    pivot_block = lax.dot_general(
        placing, aside[:, 0:piv], over_first, precision=lax.Precision.HIGHEST,
        preferred_element_type=jnp.float32,
    )
    gram = lax.dot_general(picked, picked, over_last, preferred_element_type=jnp.float32)
    sub = lax.broadcasted_iota(jnp.int32, (piv, piv), 0)
    lan = lax.broadcasted_iota(jnp.int32, (piv, piv), 1)
    eye = jnp.where(sub == lan, 1.0, 0.0)
    state = jnp.concatenate([pivot_block - gram, eye], axis=1)
    sub_col = lax.broadcasted_iota(jnp.int32, (piv, 1), 0)
    every = max(1, piv // parts)
    done = 0

    def subtract(i):
        at = slice(i * part, (i + 1) * part)
        new[:, at] = col[:, at] - dot_t(picked, vec[at, :])

    for k in range(piv):
        scale = 1.0 / state[k : k + 1, k : k + 1]
        mult = jnp.where(sub_col > k, state[:, k : k + 1] * scale, 0.0)
        state = state - mult * state[k : k + 1, :]
        if k % every == every - 1 and done < parts:
            subtract(done)
            done += 1
    for i in range(done, parts):
        subtract(i)
    diag = jnp.sum(jnp.where(sub == lan, state[:, 0:piv], 0.0), axis=1, keepdims=True)
    inverse = state[:, piv : 2 * piv] * lax.rsqrt(diag)
    inv_hi, rest = split(inverse)
    inv_lo = rest.astype(jnp.bfloat16)
    wide = jnp.concatenate([inv_hi, inv_lo, inv_hi, inv_lo], axis=1)
    for i in range(parts):
        at = slice(i * part, (i + 1) * part)
        rem_hi, rest = split(new[:, at])
        rem_lo = rest.astype(jnp.bfloat16)
        tall = jnp.concatenate([rem_hi, rem_hi, rem_lo, rem_lo], axis=0)
        value = jnp.dot(wide, tall, preferred_element_type=jnp.float32)
        for s in range(i * part // block, (i + 1) * part // block):
            lane = slice(s * block - i * part, (s + 1) * block - i * part)
            kept = jnp.where(live_col[s : s + 1, :] > 0, value[:, lane], 0.0)
            new[:, s * block : (s + 1) * block] = kept
            sums[s : s + 1, :] = jnp.sum(kept * kept, axis=0, keepdims=True)
    out_copy = pltpu.make_async_copy(new, new_hbm, out_sem)
    out_copy.start()

    alive = jnp.broadcast_to(live_col, (slots, block)) > 0
    updated = res_ref[...] - jnp.where(alive, sums[...], 0.0)
    updated = jnp.where(marks[...] > 0.0, 0.0, updated)
    best = jnp.max(jnp.where(alive, updated, 0.0), axis=(0, 1), keepdims=True)
    mine[...] = jnp.broadcast_to(best, mine.shape)

    def tell(t, carry):
        pltpu.make_async_remote_copy(
            src_ref=mine, dst_ref=tops.at[me], send_sem=top_send, recv_sem=top_recv,
            device_id=place(lax.rem(me + t, n)), device_id_type=MESH,
        ).start()
        return carry

    lax.fori_loop(1, n, tell, 0)
    top_own = pltpu.make_async_copy(mine, tops.at[me], own_sem)
    top_own.start()
    top_own.wait()
    others = pltpu.make_async_remote_copy(
        src_ref=tops.at[pl.ds(0, n - 1)], dst_ref=tops.at[pl.ds(0, n - 1)],
        send_sem=top_send, recv_sem=top_recv,
        device_id=(my_row, partner_grp), device_id_type=MESH,
    )
    others.wait_recv()
    peak = jnp.max(jnp.max(tops[...], axis=0), axis=1, keepdims=True)
    peak_ref[...] = peak
    rel_ref[...] = updated / peak
    others.wait_send()
    pltpu.make_async_remote_copy(
        src_ref=half_ref, dst_ref=half_ref, send_sem=send_sem, recv_sem=core_sem,
        device_id=(my_row, partner_grp), device_id_type=MESH,
    ).wait_send()
    rest_ref = got.at[pl.ds(0, (half - 1) * rows_sent), :]
    pltpu.make_async_remote_copy(
        src_ref=rest_ref, dst_ref=rest_ref, send_sem=send_sem, recv_sem=core_sem,
        device_id=(my_row, partner_grp), device_id_type=MESH,
    ).wait_send()
    out_copy.wait()


def solution(mesh):
    n_rows, n_grp = mesh.shape["rows"], mesh.shape["grp"]
    n = n_rows * n_grp

    def on_device(vectors, columns, residual, slot_block, live, pivots):
        total, depth = vectors.shape
        slots = slot_block.shape[0]
        block = total // slots
        piv = pivots.shape[0]
        per = max(1, piv // n)
        chunks = depth // LANES
        part = 2 * block if slots % 2 == 0 else block
        rows_sent = -(-(per * (chunks + 1)) // 8) * 8
        hbm = pl.BlockSpec(memory_space=pl.ANY)
        vmem = pl.BlockSpec(memory_space=pltpu.VMEM)
        smem = pl.BlockSpec(memory_space=pltpu.SMEM)
        dma = pltpu.SemaphoreType.DMA
        new, rel, peak = pl.pallas_call(
            functools.partial(step_kernel, (n_rows, n_grp, per, block, rows_sent, part)),
            out_shape=(
                jax.ShapeDtypeStruct((piv, total), jnp.float32),
                jax.ShapeDtypeStruct((slots, block), jnp.float32),
                jax.ShapeDtypeStruct((1, 1), jnp.float32),
            ),
            in_specs=[hbm, hbm, vmem, vmem, vmem, vmem],
            out_specs=(hbm, vmem, vmem),
            scratch_shapes=[
                pltpu.VMEM((total, depth), jnp.bfloat16),
                pltpu.VMEM((piv, total), jnp.float32),
                pltpu.VMEM((piv, total), jnp.float32),
                pltpu.VMEM((rows_sent, LANES), jnp.float32),
                pltpu.VMEM((n * rows_sent, LANES), jnp.float32),
                pltpu.VMEM((1, LANES), jnp.float32),
                pltpu.VMEM((n, 1, LANES), jnp.float32),
                pltpu.VMEM((slots, block), jnp.float32),
                pltpu.VMEM((slots, block), jnp.float32),
                dma((total // part,)), dma, dma, dma, dma((n // 2,)), dma, dma, dma, dma,
            ],
            compiler_params=pltpu.CompilerParams(
                collective_id=0, has_side_effects=True, vmem_limit_bytes=48 << 20
            ),
        )(
            vectors, columns.T, residual.reshape(slots, block), slot_block.reshape(1, slots),
            live.reshape(1, slots), pivots.reshape(1, piv),
        )
        return new.T, rel.reshape(total), peak.reshape(())

    spread = P(("rows", "grp"))
    return jax.shard_map(
        on_device,
        mesh=mesh,
        in_specs=(P(("rows", "grp"), None), P(("rows", "grp"), None), spread, spread, spread, P()),
        out_specs=(P(("rows", "grp"), None), spread, P()),
        check_vma=False,
    )
```

time: 195 us -> 37.5 us (0.19)
  blocking collectives: 157 us -> 0 us
  Pallas kernels: 0 us -> 29.8 us
  other arithmetic: 18.2 us -> 0 us
  matrix products: 9.07 us -> 0 us
  local copies, waits for them, and re-layouts: 8.06 us -> 5.09 us
    all_gather x2 -> x0, blocking collectives: 78.4 us -> none  [the longest x1 41.7 us: on_device(): lax.all_gather(packed_vectors, ('rows', 'grp'), axis=0, tiled=True)]
    unnamed x1 -> x0, blocking collectives: 42 us -> none
    pmax x1 -> x0, blocking collectives: 37.1 us -> none  [on_device(): peak = lax.pmax(local_peak, ('rows', 'grp'))]
    pallas_call x0 -> x1, Pallas kernels: none -> 29.8 us  [on_device(): pl.pallas_call(functools.partial(step_kernel, (n_rows, n_grp, per, block,...]
    another operation x7 -> x0, other arithmetic: 13.4 us -> none  [the longest x3 6.52 us: on_device(): lower_factor = jnp.linalg.cholesky(pivot_block - gram)]
    dot_general x6 -> x0, matrix products: 7.63 us -> none  [the longest x1 6.04 us: on_device(): jnp.dot(cholesky_vectors, picked.T, preferred_element_type=jnp.float32)]
    gather x2 -> x0, local copies, waits for them, and re-layouts: 6.05 us -> none  [the longest x1 5.45 us: on_device(): cholesky_vectors[local_row]]
    unnamed x9 -> x12, local copies, waits for them, and re-layouts: 1.76 us -> 5.09 us
where the time goes in v1:
time: 37.5 us; the launch traced here: 37.2 us
  Pallas kernels  29.8 us (79%)
  local copies, waits for them, and re-layouts  5.09 us (14%)
  between operations  2.34 us (6%)
    pallas_call x1, Pallas kernels, on_device(): pl.pallas_call(functools.partial(step_kernel, (n_rows, n_grp, per, block,...  29.8 us
    unnamed x12, local copies, waits for them, and re-layouts  5.09 us

profile of v1, /device:TPU:0, one launch (start us, length us, event | category | flops | bytes accessed | tf_op | source)
XLA Modules:
  0.0 37.2 jit_solution(1593384646603529179)
XLA Ops:
  0.6 0.0 copy-start
  0.6 1.0 %copy-done = f32[2048,64]{0,1:T(8,128)S(1)} copy-done((f32[2048,64]{0,1:T(8,128)S(1)}, f32[2048,64]{0,1:T(8,128)}, u32[]{:S(2)}) %copy-start) | copy-done | bytes 524312
  1.7 0.0 copy-start.1
  1.7 0.7 %copy-done.1 = f32[2048]{0:T(1024)S(1)} copy-done((f32[2048]{0:T(1024)S(1)}, f32[2048]{0:T(1024)}, u32[]{:S(2)}) %copy-start.1) | copy-done | bytes 8216
  2.4 0.0 copy-start.2
  2.4 0.7 %copy-done.2 = s32[16]{0:T(128)S(1)} copy-done((s32[16]{0:T(128)S(1)}, s32[16]{0:T(128)}, u32[]{:S(2)}) %copy-start.2) | copy-done | bytes 88
  3.0 0.0 copy-start.3
  3.0 0.7 %copy-done.3 = s32[16]{0:T(128)S(1)} copy-done((s32[16]{0:T(128)S(1)}, s32[16]{0:T(128)}, u32[]{:S(2)}) %copy-start.3) | copy-done | bytes 88
  3.7 0.0 copy-start.4
  3.7 0.7 %copy-done.4 = s32[64]{0:T(128)S(1)} copy-done((s32[64]{0:T(128)S(1)}, s32[64]{0:T(128)}, u32[]{:S(2)}) %copy-start.4) | copy-done | bytes 280
  4.3 29.8 %shard_map.85 = (f32[64,2048]{1,0:T(8,128)S(1)}, f32[16,128]{1,0:T(8,128)S(1)}, f32[1,1]{1,0:T(1,128)}) custom-call(bf16[2048,2048]{1,0:T(8,128)(2,1)} %vec_hbm.1, f32[64,2048]{1,0:T(8,128)S(1)} %bitcast.8, f32[16,128]{1,0:T(8,128)S(1)} %bitcast.11, s32[1,16]{1,0:T(1,128)S(1)} %bitcast.12, s32[1,16]{1,0:T(1,128)S(1)} %bitcast.13, s32[1,64]{1,0:T(1,128)S(1)} %bitcast.14), custom_call_target="tpu_custom_call" | custom-call | tf_op jit(solution)/shard_map/pallas_call | solution.py:285
  34.1 0.8 %copy.12 = f32[2048,64]{0,1:T(8,128)} copy(f32[2048,64]{0,1:T(8,128)S(1)} %bitcast.9) | data formatting | bytes 1048576
  34.9 0.6 %copy.13 = f32[2048]{0:T(1024)} copy(f32[2048]{0:T(1024)S(1)} %bitcast.10) | data formatting | bytes 16384
Async XLA Ops:
  0.6 1.0 %copy-start = (f32[2048,64]{0,1:T(8,128)S(1)}, f32[2048,64]{0,1:T(8,128)}, u32[]{:S(2)}) copy-start(f32[2048,64]{0,1:T(8,128)} %param.7) | copy-start | bytes 1572868
  1.7 0.7 %copy-start.1 = (f32[2048]{0:T(1024)S(1)}, f32[2048]{0:T(1024)}, u32[]{:S(2)}) copy-start(f32[2048]{0:T(1024)} %param.8) | copy-start | bytes 24580
  2.4 0.7 %copy-start.2 = (s32[16]{0:T(128)S(1)}, s32[16]{0:T(128)}, u32[]{:S(2)}) copy-start(s32[16]{0:T(128)} %param.9) | copy-start | bytes 196
  3.0 0.7 %copy-start.3 = (s32[16]{0:T(128)S(1)}, s32[16]{0:T(128)}, u32[]{:S(2)}) copy-start(s32[16]{0:T(128)} %param.10) | copy-start | bytes 196
  3.7 0.7 %copy-start.4 = (s32[64]{0:T(128)S(1)}, s32[64]{0:T(128)}, u32[]{:S(2)}) copy-start(s32[64]{0:T(128)} %param.11) | copy-start | bytes 772

commit v2 on v1

--- a/solution.py
+++ b/solution.py
@@ -12,10 +12,10 @@
 
 
 def step_kernel(
-    sizes, vec_hbm, col_hbm, res_ref, slot_ref, live_ref, piv_ref,
-    new_hbm, rel_ref, peak_ref,
-    vec, col, new, send, got, mine, tops, sums, marks,
-    vec_sem, col_sem, own_sem, send_sem, chip_sem, core_sem, top_send, top_recv, out_sem,
+    sizes, vec_hbm, col_hbm, res_hbm, slot_hbm, live_hbm, piv_hbm,
+    new_hbm, rel_hbm, peak_hbm,
+    vec, col, res_ref, slot_ref, live_ref, piv_ref, new, rel_ref, peak_ref, send, got, mine, tops, sums, marks,
+    small_sem, vec_sem, col_sem, own_sem, send_sem, chip_sem, core_sem, top_send, top_recv, out_sem,
 ):
     n_rows, n_grp, per, block, rows_sent, part = sizes
     n = n_rows * n_grp
@@ -24,6 +24,7 @@
     piv = col.shape[0]
     chunks = depth // LANES
     parts = total // part
+    used = per * (chunks + 1)
     my_row, my_grp = lax.axis_index("rows"), lax.axis_index("grp")
     me = my_row * n_grp + my_grp
     side = lax.rem(my_grp, 2)
@@ -43,8 +44,15 @@
         hi = x.astype(jnp.bfloat16)
         return hi, x - hi.astype(jnp.float32)
 
+    small_copies = [
+        pltpu.make_async_copy(source, target, small_sem.at[i])
+        for i, (source, target) in enumerate(
+            ((piv_hbm, piv_ref), (slot_hbm, slot_ref), (live_hbm, live_ref), (res_hbm, res_ref))
+        )
+    ]
+    for copy in small_copies:
+        copy.start()
     col_copy = pltpu.make_async_copy(col_hbm, col, col_sem)
-    col_copy.start()
     vec_copies = [
         pltpu.make_async_copy(
             vec_hbm.at[pl.ds(i * part, part), :], vec.at[pl.ds(i * part, part), :], vec_sem.at[i]
@@ -53,6 +61,7 @@
     ]
     for copy in vec_copies:
         copy.start()
+    col_copy.start()
 
     barrier = pltpu.get_barrier_semaphore()
 
@@ -72,6 +81,8 @@
             jnp.where(iota((size, size), 0) == iota((size, size), 1), row, 0), axis=1, keepdims=True
         )
 
+    for copy in small_copies:
+        copy.wait()
     piv_row = piv_ref[...]
     slot_row = slot_ref[...]
     piv_col = upright(piv_row, piv)
@@ -117,15 +128,15 @@
     pl.semaphore_wait(barrier, n - 1)
 
     def slot_of(flat):
-        return got.at[pl.ds(pl.multiple_of(flat * rows_sent, 8), rows_sent), :]
-
-    own_copy = pltpu.make_async_copy(send, slot_of(me), own_sem)
+        return got.at[pl.ds(pl.multiple_of(flat * rows_sent, 8), used), :]
+
+    own_copy = pltpu.make_async_copy(send.at[pl.ds(0, used), :], slot_of(me), own_sem)
     own_copy.start()
 
     def to_chip(chip):
         flat = chip * 2 + side
         return pltpu.make_async_remote_copy(
-            src_ref=send, dst_ref=slot_of(me), send_sem=send_sem, recv_sem=chip_sem.at[my_chip],
+            src_ref=send.at[pl.ds(0, used), :], dst_ref=slot_of(me), send_sem=send_sem, recv_sem=chip_sem.at[my_chip],
             device_id=place(flat), device_id_type=MESH,
         )
 
@@ -135,7 +146,7 @@
 
     lax.fori_loop(1, half, send_chip, 0)
     pltpu.make_async_remote_copy(
-        src_ref=send, dst_ref=slot_of(me), send_sem=send_sem, recv_sem=core_sem,
+        src_ref=send.at[pl.ds(0, used), :], dst_ref=slot_of(me), send_sem=send_sem, recv_sem=core_sem,
         device_id=(my_row, partner_grp), device_id_type=MESH,
     ).start()
 
@@ -143,7 +154,7 @@
         chip = lax.rem(my_chip + half - t, half)
         flat = chip * 2 + side
         pltpu.make_async_remote_copy(
-            src_ref=send, dst_ref=slot_of(flat), send_sem=send_sem, recv_sem=chip_sem.at[chip],
+            src_ref=send.at[pl.ds(0, used), :], dst_ref=slot_of(flat), send_sem=send_sem, recv_sem=chip_sem.at[chip],
             device_id=(my_row, partner_grp), device_id_type=MESH,
         ).wait_recv()
         pltpu.make_async_remote_copy(
@@ -153,7 +164,7 @@
         return carry
 
     lax.fori_loop(1, half, relay, 0)
-    half_ref = got.at[pl.ds(0, half * rows_sent), :]
+    half_ref = got.at[pl.ds(0, half * used), :]
     own_copy.wait()
     pltpu.make_async_remote_copy(
         src_ref=half_ref, dst_ref=half_ref, send_sem=send_sem, recv_sem=core_sem,
@@ -186,11 +197,12 @@
         preferred_element_type=jnp.float32,
     )
     gram = lax.dot_general(picked, picked, over_last, preferred_element_type=jnp.float32)
-    sub = lax.broadcasted_iota(jnp.int32, (piv, piv), 0)
-    lan = lax.broadcasted_iota(jnp.int32, (piv, piv), 1)
+    sub, lan = iota((piv, piv), 0), iota((piv, piv), 1)
     eye = jnp.where(sub == lan, 1.0, 0.0)
     state = jnp.concatenate([pivot_block - gram, eye], axis=1)
-    sub_col = lax.broadcasted_iota(jnp.int32, (piv, 1), 0)
+    tile = 8
+    bands = [state[t : t + tile, :] for t in range(0, piv, tile)]
+    sub_col = iota((tile, 1), 0)
     every = max(1, piv // parts)
     done = 0
 
@@ -198,9 +210,11 @@
         at = slice(i * part, (i + 1) * part)
         new[:, at] = col[:, at] - dot_t(picked, vec[at, :])
 
+    state = jnp.concatenate(bands, axis=0)
+    wide_col = iota((piv, 1), 0)
     for k in range(piv):
         scale = 1.0 / state[k : k + 1, k : k + 1]
-        mult = jnp.where(sub_col > k, state[:, k : k + 1] * scale, 0.0)
+        mult = jnp.where(wide_col > k, state[:, k : k + 1] * scale, 0.0)
         state = state - mult * state[k : k + 1, :]
         if k % every == every - 1 and done < parts:
             subtract(done)
@@ -223,8 +237,14 @@
             kept = jnp.where(live_col[s : s + 1, :] > 0, value[:, lane], 0.0)
             new[:, s * block : (s + 1) * block] = kept
             sums[s : s + 1, :] = jnp.sum(kept * kept, axis=0, keepdims=True)
-    out_copy = pltpu.make_async_copy(new, new_hbm, out_sem)
-    out_copy.start()
+
+    out_copies = [
+        pltpu.make_async_copy(source, target, out_sem.at[i])
+        for i, (source, target) in enumerate(
+            ((new, new_hbm), (rel_ref, rel_hbm), (peak_ref, peak_hbm))
+        )
+    ]
+    out_copies[0].start()
 
     alive = jnp.broadcast_to(live_col, (slots, block)) > 0
     updated = res_ref[...] - jnp.where(alive, sums[...], 0.0)
@@ -252,17 +272,41 @@
     peak = jnp.max(jnp.max(tops[...], axis=0), axis=1, keepdims=True)
     peak_ref[...] = peak
     rel_ref[...] = updated / peak
+    out_copies[1].start()
+    out_copies[2].start()
     others.wait_send()
     pltpu.make_async_remote_copy(
         src_ref=half_ref, dst_ref=half_ref, send_sem=send_sem, recv_sem=core_sem,
         device_id=(my_row, partner_grp), device_id_type=MESH,
     ).wait_send()
-    rest_ref = got.at[pl.ds(0, (half - 1) * rows_sent), :]
+    rest_ref = got.at[pl.ds(0, (half - 1) * used), :]
     pltpu.make_async_remote_copy(
         src_ref=rest_ref, dst_ref=rest_ref, send_sem=send_sem, recv_sem=core_sem,
         device_id=(my_row, partner_grp), device_id_type=MESH,
     ).wait_send()
-    out_copy.wait()
+    for copy in out_copies:
+        copy.wait()
+
+
+def finish_kernel(pieces, *refs):
+    sources, targets, buffers, (in_sem, out_sem) = refs[0:3], refs[3:6], refs[6:9], refs[9:11]
+    width = sources[0].shape[1] // pieces
+    moves = [(1, slice(None)), (2, slice(None))]
+    moves += [(0, slice(p * width, (p + 1) * width)) for p in range(pieces)]
+    ins, outs = [], []
+    for i, (which, at) in enumerate(moves):
+        source, buffer, target = (
+            side[which].at[:, at] for side in (sources, buffers, targets)
+        )
+        ins.append(pltpu.make_async_copy(source, buffer, in_sem.at[i]))
+        outs.append(pltpu.make_async_copy(buffer, target, out_sem.at[i]))
+    for copy in ins:
+        copy.start()
+    for arriving, leaving in zip(ins, outs):
+        arriving.wait()
+        leaving.start()
+    for copy in outs:
+        copy.wait()
 
 
 def solution(mesh):
@@ -278,38 +322,53 @@
         chunks = depth // LANES
         part = 2 * block if slots % 2 == 0 else block
         rows_sent = -(-(per * (chunks + 1)) // 8) * 8
-        hbm = pl.BlockSpec(memory_space=pl.ANY)
-        vmem = pl.BlockSpec(memory_space=pltpu.VMEM)
-        smem = pl.BlockSpec(memory_space=pltpu.SMEM)
+        hbm = pl.BlockSpec(memory_space=pltpu.HBM)
         dma = pltpu.SemaphoreType.DMA
+        shapes = (
+            jax.ShapeDtypeStruct((piv, total), jnp.float32),
+            jax.ShapeDtypeStruct((slots, block), jnp.float32),
+            jax.ShapeDtypeStruct((1, 1), jnp.float32),
+        )
         new, rel, peak = pl.pallas_call(
             functools.partial(step_kernel, (n_rows, n_grp, per, block, rows_sent, part)),
-            out_shape=(
-                jax.ShapeDtypeStruct((piv, total), jnp.float32),
-                jax.ShapeDtypeStruct((slots, block), jnp.float32),
-                jax.ShapeDtypeStruct((1, 1), jnp.float32),
-            ),
-            in_specs=[hbm, hbm, vmem, vmem, vmem, vmem],
-            out_specs=(hbm, vmem, vmem),
+            out_shape=shapes,
+            in_specs=[hbm] * 6,
+            out_specs=(hbm,) * 3,
             scratch_shapes=[
                 pltpu.VMEM((total, depth), jnp.bfloat16),
                 pltpu.VMEM((piv, total), jnp.float32),
-                pltpu.VMEM((piv, total), jnp.float32),
+                pltpu.VMEM((slots, block), jnp.float32),
+                pltpu.VMEM((1, slots), jnp.int32),
+                pltpu.VMEM((1, slots), jnp.int32),
+                pltpu.VMEM((1, piv), jnp.int32),
+                *(pltpu.VMEM(shape.shape, shape.dtype) for shape in shapes),
                 pltpu.VMEM((rows_sent, LANES), jnp.float32),
                 pltpu.VMEM((n * rows_sent, LANES), jnp.float32),
                 pltpu.VMEM((1, LANES), jnp.float32),
                 pltpu.VMEM((n, 1, LANES), jnp.float32),
                 pltpu.VMEM((slots, block), jnp.float32),
                 pltpu.VMEM((slots, block), jnp.float32),
-                dma((total // part,)), dma, dma, dma, dma((n // 2,)), dma, dma, dma, dma,
+                dma((4,)), dma((total // part,)), dma, dma, dma, dma((n // 2,)), dma, dma, dma, dma((3,)),
             ],
             compiler_params=pltpu.CompilerParams(
-                collective_id=0, has_side_effects=True, vmem_limit_bytes=48 << 20
+                collective_id=0, has_side_effects=True, vmem_limit_bytes=62 << 20
             ),
         )(
             vectors, columns.T, residual.reshape(slots, block), slot_block.reshape(1, slots),
             live.reshape(1, slots), pivots.reshape(1, piv),
         )
+        pieces = 4
+        new, rel, peak = pl.pallas_call(
+            functools.partial(finish_kernel, pieces),
+            out_shape=shapes,
+            in_specs=[hbm] * 3,
+            out_specs=(hbm,) * 3,
+            scratch_shapes=[
+                *(pltpu.VMEM(shape.shape, shape.dtype) for shape in shapes),
+                dma((pieces + 2,)), dma((pieces + 2,)),
+            ],
+            compiler_params=pltpu.CompilerParams(vmem_limit_bytes=62 << 20),
+        )(new, rel, peak)
         return new.T, rel.reshape(total), peak.reshape(())
 
     spread = P(("rows", "grp"))

time: 37.5 us -> 32.7 us (0.87)
  local copies, waits for them, and re-layouts: 5.09 us -> 0 us
  Pallas kernels: 29.8 us -> 31.8 us
  between operations: 2.34 us -> 0.64 us
    unnamed x12 -> x0, local copies, waits for them, and re-layouts: 5.09 us -> none
    pallas_call x0 -> x1, Pallas kernels: none -> 2.48 us  [on_device(): pl.pallas_call(functools.partial(finish_kernel, pieces), out_shape=shapes...]
    pallas_call x1, Pallas kernels: 29.8 us -> 29.4 us  [on_device(): pl.pallas_call(functools.partial(step_kernel, (n_rows, n_grp, per, block,...]
where the time goes in v2:
time: 32.7 us; the launch traced here: 32.5 us
  Pallas kernels  31.8 us (97%)
  between operations  0.64 us (2%)
    pallas_call x1, Pallas kernels, on_device(): pl.pallas_call(functools.partial(step_kernel, (n_rows, n_grp, per, block,...  29.4 us
    pallas_call x1, Pallas kernels, on_device(): pl.pallas_call(functools.partial(finish_kernel, pieces), out_shape=shapes...  2.48 us

profile of v2, /device:TPU:0, one launch (start us, length us, event | category | flops | bytes accessed | tf_op | source)
XLA Modules:
  0.0 32.5 jit_solution(12019379121706123278)
XLA Ops:
  0.6 29.4 %shard_map.85 = (f32[64,2048]{1,0:T(8,128)}, f32[16,128]{1,0:T(8,128)}, f32[1,1]{1,0:T(1,128)}) custom-call(bf16[2048,2048]{1,0:T(8,128)(2,1)} %vec_hbm.1, f32[64,2048]{1,0:T(8,128)} %bitcast.8, f32[16,128]{1,0:T(8,128)} %bitcast.9, s32[1,16]{1,0:T(1,128)} %bitcast.10, s32[1,16]{1,0:T(1,128)} %bitcast.11, s32[1,64]{1,0:T(1,128)} %bitcast.12), custom_call_target="tpu_custom_call" | custom-call | tf_op jit(solution)/shard_map/pallas_call | solution.py:332
  30.0 2.5 %shard_map.86 = (f32[64,2048]{1,0:T(8,128)}, f32[16,128]{1,0:T(8,128)}, f32[1,1]{1,0:T(1,128)}) custom-call(f32[64,2048]{1,0:T(8,128)} %get-tuple-element.9.refs_0_, f32[16,128]{1,0:T(8,128)} %get-tuple-element.10.refs_1_, f32[1,1]{1,0:T(1,128)} %get-tuple-element.11.refs_2_), custom_call_target="tpu_custom_call" | custom-call | tf_op jit(solution)/shard_map/pallas_call | solution.py:361
